TPU v7x, 32 devices: a whole 2x2x4 slice. The times are simulated.
32 devices in a mesh: heads: 4 (over y, x), seq: 8 (over z, core).
Axes of the slice: x: 2, y: 2, z: 4, core: 2. Of those that a mesh axis runs over, the one named last changes fastest.
Arguments:
- tokens: bfloat16 [7168, 2048], P('seq'), may hold values from -6 to 6
- w_qkv: bfloat16 [2048, 3, 2048], P(None, None, 'heads'), may hold values from -0.1875 to 0.1875
- w_out: bfloat16 [2048, 2048], P('heads'), may hold values from -0.75 to 0.75
- w_up: bfloat16 [2048, 8192], P('seq', 'heads'), may hold values from -0.125 to 0.125
- w_down: bfloat16 [8192, 2048], P('heads', 'seq'), may hold values from -0.0625 to 0.0625
- gain_attn: float32 [2048], replicated, may hold values from 0.1 to 1.9
- gain_ffn: float32 [2048], replicated, may hold values from 0.1 to 1.9
- w_router: float32 [2048, 8], replicated, may hold values from -0.25 to 0.25
- head_quarters: int32 [5], replicated, may hold values from 1 to 4, as said below
- ffn_quarters: int32 [5], replicated, may hold values from 1 to 4, as said below
- router_targets: int32 [5, 2], replicated, may hold values from 0 to 3
- cotangent: bfloat16 [7168, 2048], P('seq'), may hold values from -6 to 6
Outputs:
- output: bfloat16 [7168, 2048], P('seq')
- grad_tokens: float32 [7168, 2048], P('seq')
- grad_qkv: float32 [2048, 3, 2048], P(None, None, 'heads')
- grad_out: float32 [2048, 2048], P('heads')
- grad_up: float32 [2048, 8192], P('seq', 'heads')
- grad_down: float32 [8192, 2048], P('heads', 'seq')
- grad_gain_attn: float32 [2048], replicated
- grad_gain_ffn: float32 [2048], replicated
- grad_router: float32 [2048, 8], replicated
Inputs may be any that keep to these rules, and one draw needn't show every extreme that they name: Sequence s uses the first head_quarters[s] * 4 heads; some sequence uses all heads and some a quarter of them. Sequence s uses the first ffn_quarters[s] * 2048 hidden units; some sequence uses all and some a quarter.
All inputs are finite; a program needn't handle non-finite values.
Results may differ from a plain program's by a relative error of at most 0.023.
Values may be sent and summed in bfloat16 or wider, within the bound.
No kernel may reach another device: no remote copies, remote signals or barrier semaphores. Data moves between devices by JAX's collectives and lax.ppermute only.
A program may use at most 256 MiB of HBM per device.

v0:
```python
import jax
import jax.numpy as jnp
from jax import lax
from jax.sharding import PartitionSpec as P

D = 2048
H = 16
HD = 128
FF = 8192
SHORT_DEV = 128
NSHORT = 3
NLONG = 2
LEVELS = 4
SEQS = 5
epsilon = 1e-05
highest = lax.Precision.HIGHEST


def normalize_parts(values):
    centered = values - jnp.mean(values, axis=-1, keepdims=True)
    inverse = lax.rsqrt(jnp.mean(centered * centered, axis=-1, keepdims=True) + epsilon)
    return (centered * inverse, inverse)


def normalize_back(grad_normed, normed_hat, inverse, gain):
    grad_hat = grad_normed * gain
    middle = (
        grad_hat
        - jnp.mean(grad_hat, axis=-1, keepdims=True)
        - normed_hat * jnp.mean(grad_hat * normed_hat, axis=-1, keepdims=True)
    )
    return (inverse * middle, jnp.sum(grad_normed * normed_hat, axis=0))


def rotate(values, cosine, sine, inverse_turn):
    row_count = values.shape[0]
    shaped = values.reshape(row_count, -1, HD)
    half_dim = HD // 2
    former = shaped[..., :half_dim]
    latter = shaped[..., half_dim:]
    if inverse_turn:
        turned = [former * cosine + latter * sine, latter * cosine - former * sine]
    else:
        turned = [former * cosine - latter * sine, latter * cosine + former * sine]
    return jnp.concatenate(turned, axis=-1).reshape(row_count, -1)


def gather_rows(keys, values):
    return (
        lax.all_gather(keys, "seq", axis=1, tiled=True),
        lax.all_gather(values, "seq", axis=1, tiled=True),
    )


def masked_scores(query, keys, first_pos):
    seq_number, seq_size = (query.shape[0], query.shape[1])
    length = keys.shape[1]
    query_heads = query.reshape(seq_number, seq_size, -1, HD)
    key_heads = keys.reshape(seq_number, length, -1, HD)
    scores = jnp.einsum(
        "cqhd,ckhd->chqk", query_heads, key_heads, preferred_element_type=jnp.float32
    ) * HD ** (-0.5)
    allowed = jnp.arange(length)[None, :] <= (first_pos + jnp.arange(seq_size))[:, None]
    return (jnp.where(allowed[None, None], scores, -1e30), query_heads, key_heads)


def attend_forward(query, keys, values, first_pos):
    seq_number, seq_size = (query.shape[0], query.shape[1])
    scores, query_heads, key_heads = masked_scores(query, keys, first_pos)
    largest = jnp.max(scores, axis=-1, keepdims=True)
    raised = jnp.exp(scores - largest)
    total = jnp.sum(raised, axis=-1, keepdims=True)
    probs = (raised / total).astype(jnp.bfloat16)
    value_heads = values.reshape(seq_number, values.shape[1], -1, HD)
    mixed = jnp.einsum("chqk,ckhd->cqhd", probs, value_heads, preferred_element_type=jnp.float32)
    return (mixed.reshape(seq_number, seq_size, -1), largest + jnp.log(total))


def attend_backward(query, keys, values, grad_mixed, log_total, first_pos):
    seq_number, seq_size = (query.shape[0], query.shape[1])
    length = keys.shape[1]
    scores, query_heads, key_heads = masked_scores(query, keys, first_pos)
    probs = jnp.exp(scores - log_total)
    value_heads = values.reshape(seq_number, length, -1, HD)
    grad_heads = grad_mixed.reshape(seq_number, seq_size, -1, HD)
    grad_probs = jnp.einsum(
        "cqhd,ckhd->chqk", grad_heads, value_heads, preferred_element_type=jnp.float32
    )
    delta = jnp.sum(probs * grad_probs, axis=-1)
    grad_scores = (probs * (grad_probs - delta[..., None])).astype(jnp.bfloat16)
    grad_query = jnp.einsum(
        "chqk,ckhd->cqhd", grad_scores, key_heads, preferred_element_type=jnp.float32
    ) * HD ** (-0.5)
    grad_query = grad_query.reshape(seq_number, seq_size, -1)
    return (grad_query, delta)


def attend_key_side(query_all, keys, values, grad_all, total_all, delta_all, key_first):
    seq_number, length = (query_all.shape[0], query_all.shape[1])
    key_count = keys.shape[1]
    query_heads = query_all.reshape(seq_number, length, -1, HD)
    key_heads = keys.reshape(seq_number, key_count, -1, HD)
    value_heads = values.reshape(seq_number, key_count, -1, HD)
    grad_heads = grad_all.reshape(seq_number, length, -1, HD)
    scores = jnp.einsum(
        "cqhd,ckhd->chqk", query_heads, key_heads, preferred_element_type=jnp.float32
    ) * HD ** (-0.5)
    allowed = (key_first + jnp.arange(key_count))[None, :] <= jnp.arange(length)[:, None]
    scores = jnp.where(allowed[None, None], scores, -1e30)
    probs = jnp.exp(scores - total_all[..., None])
    probs_low = probs.astype(jnp.bfloat16)
    grad_probs = jnp.einsum(
        "cqhd,ckhd->chqk", grad_heads, value_heads, preferred_element_type=jnp.float32
    )
    grad_scores = (probs * (grad_probs - delta_all[..., None])).astype(jnp.bfloat16)
    grad_values = jnp.einsum(
        "chqk,cqhd->ckhd", probs_low, grad_heads, preferred_element_type=jnp.float32
    )
    grad_keys = jnp.einsum(
        "chqk,cqhd->ckhd", grad_scores, query_heads, preferred_element_type=jnp.float32
    ) * HD ** (-0.5)
    return (
        grad_keys.reshape(seq_number, key_count, -1),
        grad_values.reshape(seq_number, key_count, -1),
    )


def local(
    tokens,
    w_qkv,
    w_out,
    w_up,
    w_down,
    gain_attn,
    gain_ffn,
    w_router,
    head_quarters,
    ffn_quarters,
    router_targets,
    cotangent,
):
    row_count = tokens.shape[0]
    seq_rank = lax.axis_index("seq")
    seq_count = lax.axis_size("seq")
    head_rank = lax.axis_index("heads")
    head_width = w_out.shape[0]
    ffn_width = w_up.shape[1]
    short_rows = NSHORT * SHORT_DEV
    column = jnp.arange(row_count)
    is_short = column < short_rows
    offset = column - short_rows
    seq_id = jnp.where(is_short, column // SHORT_DEV, NSHORT + offset // (2 * SHORT_DEV))
    position = jnp.where(
        is_short,
        seq_rank * SHORT_DEV + column % SHORT_DEV,
        seq_rank * 2 * SHORT_DEV + offset % (2 * SHORT_DEV),
    )
    in_seq = seq_id[:, None] == jnp.arange(SEQS)[None, :]
    member = in_seq.astype(jnp.float32)
    seq_length = jnp.where(
        jnp.arange(SEQS) < NSHORT, SHORT_DEV * seq_count, 2 * SHORT_DEV * seq_count
    ).astype(jnp.float32)
    head_level = jnp.sum(jnp.where(in_seq, head_quarters[None, :], 0), axis=1)
    ffn_level = jnp.sum(jnp.where(in_seq, ffn_quarters[None, :], 0), axis=1)
    head_index = head_rank * (head_width // HD) + jnp.arange(head_width) // HD
    head_live = (head_index[None, :] < (head_level * (H // LEVELS))[:, None]).astype(jnp.bfloat16)
    unit_index = head_rank * ffn_width + jnp.arange(ffn_width)
    ffn_live = (unit_index[None, :] < (ffn_level * (FF // LEVELS))[:, None]).astype(jnp.float32)
    half_dim = HD // 2
    frequency = 10000.0 ** (-jnp.arange(half_dim, dtype=jnp.float32) * 2.0 / HD)
    angle = position.astype(jnp.float32)[:, None] * frequency[None, :]
    cosine = jnp.cos(angle)[:, None, :]
    sine = jnp.sin(angle)[:, None, :]
    tokens_wide = tokens.astype(jnp.float32)
    hat_one, inverse_one = normalize_parts(tokens_wide)
    normed_one = hat_one * gain_attn
    normed_low = normed_one.astype(jnp.bfloat16)
    flat_qkv = w_qkv.reshape(D, -1)
    projected = jnp.dot(normed_low, flat_qkv, preferred_element_type=jnp.float32).reshape(
        row_count, 3, head_width
    )
    query = rotate(projected[:, 0], cosine, sine, False).astype(jnp.bfloat16)
    keys = rotate(projected[:, 1], cosine, sine, False).astype(jnp.bfloat16)
    values = projected[:, 2].astype(jnp.bfloat16)
    partial_pool = jnp.dot(
        member.T, normed_one, precision=highest, preferred_element_type=jnp.float32
    )
    pooled = (
        lax.psum(partial_pool.astype(jnp.bfloat16), "seq").astype(jnp.float32)
        * lax.rsqrt(seq_length)[:, None]
    )
    shape_list = ((0, NSHORT, SHORT_DEV), (short_rows, NLONG, 2 * SHORT_DEV))
    saved_parts = []
    mixed_parts = []
    for row_start, seq_number, seq_size in shape_list:
        row_stop = row_start + seq_number * seq_size
        piece_query = query[row_start:row_stop].reshape(seq_number, seq_size, head_width)
        piece_keys = keys[row_start:row_stop].reshape(seq_number, seq_size, head_width)
        piece_values = values[row_start:row_stop].reshape(seq_number, seq_size, head_width)
        gathered_keys, gathered_values = gather_rows(piece_keys, piece_values)
        mixed, log_total = attend_forward(
            piece_query, gathered_keys, gathered_values, seq_rank * seq_size
        )
        saved_parts.append(
            (piece_query, piece_keys, piece_values, gathered_keys, gathered_values, log_total)
        )
        mixed_parts.append(mixed.reshape(seq_number * seq_size, head_width))
    heads_out = (jnp.concatenate(mixed_parts, axis=0) * head_live).astype(jnp.bfloat16)
    attn_part = jnp.dot(heads_out, w_out, preferred_element_type=jnp.float32)
    hidden = tokens_wide + lax.psum(attn_part, "heads")
    hat_two, inverse_two = normalize_parts(hidden)
    normed_two = (hat_two * gain_ffn).astype(jnp.bfloat16)
    full_up, full_down = (
        lax.all_gather(w_up, "seq", axis=0, tiled=True),
        lax.all_gather(w_down, "seq", axis=1, tiled=True),
    )
    upward = jnp.dot(normed_two, full_up, preferred_element_type=jnp.float32)
    active = (jnp.square(jnp.maximum(upward, 0.0)) * ffn_live).astype(jnp.bfloat16)
    ffn_part = jnp.dot(active, full_down, preferred_element_type=jnp.float32)
    output = (hidden + lax.psum(ffn_part.astype(jnp.bfloat16), "heads").astype(jnp.float32)).astype(
        jnp.bfloat16
    )
    back_up, back_down = (
        lax.all_gather(w_up, "seq", axis=0, tiled=True),
        lax.all_gather(w_down, "seq", axis=1, tiled=True),
    )
    upward_again = jnp.dot(normed_two, back_up, preferred_element_type=jnp.float32)
    active_again = (jnp.square(jnp.maximum(upward_again, 0.0)) * ffn_live).astype(jnp.bfloat16)
    grad_active = jnp.dot(cotangent, back_down.T, preferred_element_type=jnp.float32).astype(
        jnp.bfloat16
    )
    grad_upward = (
        grad_active.astype(jnp.float32) * ffn_live * 2.0 * jnp.maximum(upward_again, 0.0)
    ).astype(jnp.bfloat16)
    grad_down_part = jnp.dot(active_again.T, cotangent, preferred_element_type=jnp.float32)
    grad_up_part = jnp.dot(normed_two.T, grad_upward, preferred_element_type=jnp.float32)
    grad_two = lax.psum(
        jnp.dot(grad_upward, back_up.T, preferred_element_type=jnp.float32), "heads"
    )
    grad_up, grad_down = (
        lax.psum_scatter(
            grad_up_part.astype(jnp.bfloat16), "seq", scatter_dimension=0, tiled=True
        ).astype(jnp.float32),
        lax.psum_scatter(
            grad_down_part.astype(jnp.bfloat16), "seq", scatter_dimension=1, tiled=True
        ).astype(jnp.float32),
    )
    back_two, grad_gain_two = normalize_back(grad_two, hat_two, inverse_two, gain_ffn)
    grad_hidden = cotangent.astype(jnp.float32) + back_two
    grad_attn = grad_hidden.astype(jnp.bfloat16)
    grad_out_part = jnp.dot(heads_out.T, grad_attn, preferred_element_type=jnp.float32)
    grad_heads = (
        jnp.dot(grad_attn, w_out.T, preferred_element_type=jnp.float32).astype(jnp.bfloat16)
        * head_live
    )
    query_grads = []
    key_grads = []
    value_grads = []
    for shape_entry, saved in zip(shape_list, saved_parts):
        row_start, seq_number, seq_size = shape_entry
        piece_query, piece_keys, piece_values, gathered_keys, gathered_values, log_total = saved
        piece_grad = grad_heads[row_start : row_start + seq_number * seq_size].reshape(
            seq_number, seq_size, head_width
        )
        grad_query, delta = attend_backward(
            piece_query, gathered_keys, gathered_values, piece_grad, log_total, seq_rank * seq_size
        )
        query_all, grad_all = (
            lax.all_gather(piece_query, "seq", axis=1, tiled=True),
            lax.all_gather(piece_grad, "seq", axis=1, tiled=True),
        )
        total_all, delta_all = (
            lax.all_gather(log_total[..., 0], "seq", axis=2, tiled=True),
            lax.all_gather(delta, "seq", axis=2, tiled=True),
        )
        local_keys, local_values = attend_key_side(
            query_all, piece_keys, piece_values, grad_all, total_all, delta_all, seq_rank * seq_size
        )
        query_grads.append(grad_query.reshape(seq_number * seq_size, head_width))
        key_grads.append(local_keys.reshape(seq_number * seq_size, head_width))
        value_grads.append(local_values.reshape(seq_number * seq_size, head_width))
    grad_query_all = rotate(jnp.concatenate(query_grads, axis=0), cosine, sine, True)
    grad_key_all = rotate(jnp.concatenate(key_grads, axis=0), cosine, sine, True)
    grad_value_all = jnp.concatenate(value_grads, axis=0)
    grad_projected = (
        jnp.stack([grad_query_all, grad_key_all, grad_value_all], axis=1)
        .astype(jnp.bfloat16)
        .reshape(row_count, -1)
    )
    grad_qkv_part = jnp.dot(
        normed_low.T, grad_projected, preferred_element_type=jnp.float32
    ).reshape(D, 3, head_width)
    grad_one = lax.psum(
        jnp.dot(grad_projected, flat_qkv.T, preferred_element_type=jnp.float32).astype(
            jnp.bfloat16
        ),
        "heads",
    ).astype(jnp.float32)
    logits = jnp.dot(pooled, w_router, precision=highest, preferred_element_type=jnp.float32)
    logit_grads = []
    for group in range(2):
        group_logits = logits[:, LEVELS * group : LEVELS * (group + 1)]
        raised = jnp.exp(group_logits - jnp.max(group_logits, axis=1, keepdims=True))
        chosen = (jnp.arange(LEVELS)[None, :] == router_targets[:, group][:, None]).astype(
            jnp.float32
        )
        logit_grads.append(raised / jnp.sum(raised, axis=1, keepdims=True) - chosen)
    grad_logits = jnp.concatenate(logit_grads, axis=1)
    grad_router = jnp.dot(
        pooled.T, grad_logits, precision=highest, preferred_element_type=jnp.float32
    )
    grad_pooled = (
        jnp.dot(grad_logits, w_router.T, precision=highest, preferred_element_type=jnp.float32)
        * lax.rsqrt(seq_length)[:, None]
    )
    grad_one = grad_one + jnp.dot(
        member, grad_pooled, precision=highest, preferred_element_type=jnp.float32
    )
    back_one, grad_gain_one = normalize_back(grad_one, hat_one, inverse_one, gain_attn)
    grad_tokens = grad_hidden + back_one
    grad_qkv, grad_out, grad_gain_attn, grad_gain_ffn = (
        lax.psum(grad_qkv_part.astype(jnp.bfloat16), "seq").astype(jnp.float32),
        lax.psum(grad_out_part.astype(jnp.bfloat16), "seq").astype(jnp.float32),
        lax.psum(grad_gain_one.astype(jnp.bfloat16), "seq").astype(jnp.float32),
        lax.psum(grad_gain_two.astype(jnp.bfloat16), "seq").astype(jnp.float32),
    )
    return (
        output,
        grad_tokens,
        grad_qkv,
        grad_out,
        grad_up,
        grad_down,
        grad_gain_attn,
        grad_gain_ffn,
        grad_router,
    )


def solution(mesh):
    return jax.shard_map(
        local,
        mesh=mesh,
        in_specs=(
            P("seq", None),
            P(None, None, "heads"),
            P("heads", None),
            P("seq", "heads"),
            P("heads", "seq"),
            P(),
            P(),
            P(),
            P(),
            P(),
            P(),
            P("seq", None),
        ),
        out_specs=(
            P("seq", None),
            P("seq", None),
            P(None, None, "heads"),
            P("heads", None),
            P("seq", "heads"),
            P("heads", "seq"),
            P(),
            P(),
            P(),
        ),
        check_vma=False,
    )
```

profile of v0, /device:TPU:0, one launch (start us, length us, event | category | flops | bytes accessed | tf_op | source)
XLA Modules:
  0.0 1484.3 jit_solution(1231842556310068782)
XLA Ops:
  81.1 34.7 %all-gather.13.cloned.1.call-done = bf16[3,1024,512]{2,1,0:T(8,128)(2,1)} async-done(((bf16[3,128,512]{2,1,0:T(8,128)(2,1)}), bf16[3,1024,512]{2,1,0:T(8,128)(2,1)}) %all-gather.13.cloned.1.call-update) | async-done | bytes 3145744 | tf_op jit(solution)/shard_map/all_gather | solution.py:50
  134.2 29.5 %all-gather.17.cloned.1.call-done = bf16[2,2048,512]{2,1,0:T(8,128)(2,1)} async-done(((bf16[2,256,512]{2,1,0:T(8,128)(2,1)}), bf16[2,2048,512]{2,1,0:T(8,128)(2,1)}) %all-gather.17.cloned.1.call-update) | async-done | bytes 4194320 | tf_op jit(solution)/shard_map/all_gather | solution.py:50
  185.6 25.3 %all-gather.15.cloned.1.call-done = bf16[2,2048,512]{2,1,0:T(8,128)(2,1)} async-done(((bf16[2,256,512]{2,1,0:T(8,128)(2,1)}), bf16[2,2048,512]{2,1,0:T(8,128)(2,1)}) %all-gather.15.cloned.1.call-update) | async-done | bytes 4194320 | tf_op jit(solution)/shard_map/all_gather | solution.py:51
  240.7 153.0 %all-reduce.8.cloned.1.call-done = f32[896,2048]{1,0:T(8,128)} async-done(((f32[896,2048]{1,0:T(8,128)}), f32[896,2048]{1,0:T(8,128)}) %all-reduce.8.cloned.1.call-update) | async-done | bytes 7340048 | tf_op jit(solution)/shard_map/psum | solution.py:210
  402.5 74.7 %all-gather.19.cloned.1.call-done = bf16[2048,2048]{1,0:T(8,128)(2,1)} async-done(((bf16[256,2048]{1,0:T(8,128)(2,1)}), bf16[2048,2048]{1,0:T(8,128)(2,1)}) %all-gather.19.cloned.1.call-update) | async-done | bytes 8388624 | tf_op jit(solution)/shard_map/all_gather | solution.py:214
  477.2 14.6 fusion.154
  491.8 67.9 %all-gather.21.cloned.1.call-done = bf16[2048,2048]{1,0:T(8,128)(2,1)} async-done(((bf16[2048,256]{1,0:T(8,128)(2,1)}), bf16[2048,2048]{1,0:T(8,128)(2,1)}) %all-gather.21.cloned.1.call-update) | async-done | bytes 8388624 | tf_op jit(solution)/shard_map/all_gather | solution.py:215
  559.8 15.0 %fusion.29 = bf16[896,2048]{1,0:T(8,128)(2,1)} fusion(f32[896,2048]{1,0:T(8,128)} %fusion.154, s32[2048]{0:T(1024)S(1)} %iota_add_fusion, s32[896]{0:T(1024)S(1)} %broadcast_multiply_fusion, bf16[896,2048]{1,0:T(8,128)(2,1)} %param.23, bf16[2048,2048]{1,0:T(8,128)(2,1)} %all-gather.21.cloned.1.call-done), kind=kOutput, calls=%fused_computation.42 | convolution fusion | flops 7530872832 | bytes 23080448 | tf_op jit(solution)/shard_map/dot_general | solution.py:229
  593.4 146.5 %all-reduce.10.cloned.1.call-done = f32[896,2048]{1,0:T(8,128)} async-done(((f32[896,2048]{1,0:T(8,128)}), f32[896,2048]{1,0:T(8,128)}) %all-reduce.10.cloned.1.call-update) | async-done | bytes 7340048 | tf_op jit(solution)/shard_map/psum | solution.py:237
  760.6 15.4 %convolution_convert_fusion = bf16[2048,2048]{1,0:T(8,128)(2,1)} fusion(bf16[896,2048]{1,0:T(8,128)(2,1)} %param.23, f32[896,2048]{1,0:T(8,128)} %fusion.154, s32[2048]{0:T(1024)S(1)} %copy-done.58, s32[896]{0:T(1024)S(1)} %copy-done.63), kind=kOutput, calls=%fused_computation.31 | convolution fusion | flops 7529562112 | bytes 19410432 | tf_op jit(solution)/shard_map/dot_general | solution.py:235
  776.1 15.1 %convolution_convert_fusion.1 = bf16[2048,2048]{1,0:T(8,128)(2,1)} fusion(bf16[896,2048]{1,0:T(8,128)(2,1)} %fusion.29, f32[896,2048]{1,0:T(8,128)} %copy-done.3, f32[2048]{0:T(1024)S(1)} %copy-done.45, f32[896]{0:T(1024)S(1)} %add_rsqrt_fusion, f32[896]{0:T(1024)S(1)} %broadcast_multiply_fusion.6), kind=kOutput, calls=%fused_computation.32 | convolution fusion | flops 7527727104 | bytes 19414016 | tf_op jit(solution)/shard_map/dot_general | solution.py:236
  799.9 14.7 all_gather.51
  833.7 15.8 %all_gather.55 = f32[2,4,2048]{2,1,0:T(4,128)} all-gather(f32[2,4,256]{2,1,0:T(4,128)S(1)} %bitcast.162), channel_id=1, replica_groups=mesh['heads'=4,'seq'=8] {'seq'}, dimensions={2}, use_global_device_ids=true | all-gather | bytes 73728 | tf_op jit(solution)/shard_map/all_gather | solution.py:273
  872.7 13.8 multiply_reduce_fusion
  886.5 14.8 fusion.74
  901.6 15.1 %all_gather.53 = f32[3,4,1024]{2,1,0:T(4,128)S(1)} all-gather(f32[3,4,128]{2,1,0:T(4,128)S(1)} %get-tuple-element.61), channel_id=1, replica_groups=mesh['heads'=4,'seq'=8] {'seq'}, dimensions={2}, use_global_device_ids=true | all-gather | bytes 55296 | tf_op jit(solution)/shard_map/all_gather | solution.py:274
  916.7 15.4 %all_gather.57 = f32[2,4,2048]{2,1,0:T(4,128)} all-gather(f32[2,4,256]{2,1,0:T(4,128)S(1)} %get-tuple-element.59), channel_id=1, replica_groups=mesh['heads'=4,'seq'=8] {'seq'}, dimensions={2}, use_global_device_ids=true | all-gather | bytes 73728 | tf_op jit(solution)/shard_map/all_gather | solution.py:274
  966.0 13.0 fusion.72
  1010.4 15.1 %convolution_convert_fusion.3 = bf16[896,2048]{1,0:T(8,128)(2,1)} fusion(bf16[2048,2048]{1,0:T(8,128)(2,1)} %all-gather.21.cloned.1.call-done, f32[896,2048]{1,0:T(8,128)} %fusion.154, s32[2048]{0:T(1024)S(1)} %copy-done.59, s32[896]{0:T(1024)S(1)} %copy-done.64), kind=kOutput, calls=%fused_computation.73 | convolution fusion | flops 7527202816 | bytes 19410432 | tf_op jit(solution)/shard_map/dot_general | solution.py:219
  1041.9 28.2 %psum.67 = bf16[5,2048]{1,0:T(8,128)(2,1)S(1)} all-reduce(bf16[5,2048]{1,0:T(8,128)(2,1)S(1)} %fusion.55), channel_id=1, replica_groups=mesh['heads'=4,'seq'=8] {'seq'}, use_global_device_ids=true, to_apply=%region_18.19 | all-reduce | flops 10240 | bytes 40960 | tf_op jit(solution)/shard_map/psum | solution.py:189
  1074.9 22.1 %reduce-scatter.3.cloned.1.call-done = bf16[256,2048]{1,0:T(8,128)(2,1)} async-done(((bf16[2048,2048]{1,0:T(8,128)(2,1)}), bf16[256,2048]{1,0:T(8,128)(2,1)}) %reduce-scatter.3.cloned.1.call-update) | async-done | bytes 1048592 | tf_op jit(solution)/shard_map/reduce_scatter | solution.py:241
  1099.8 173.5 %all-reduce.12.cloned.1.call-done = (bf16[2048,3,512]{2,0,1:T(8,128)(2,1)}, bf16[512,2048]{1,0:T(8,128)(2,1)}) async-done(((bf16[2048,3,512]{2,0,1:T(8,128)(2,1)}, bf16[512,2048]{1,0:T(8,128)(2,1)}), (bf16[2048,3,512]{2,0,1:T(8,128)(2,1)}, bf16[512,2048]{1,0:T(8,128)(2,1)})) %all-reduce.12.cloned.1.call-update) | async-done | bytes 8388624 | tf_op jit(solution)/shard_map/psum | solution.py:322
  1284.8 148.0 %all-reduce.14.cloned.1.call-done = (bf16[896,2048]{1,0:T(8,128)(2,1)}, bf16[896,2048]{1,0:T(8,128)(2,1)}) async-done(((bf16[896,2048]{1,0:T(8,128)(2,1)}, bf16[896,2048]{1,0:T(8,128)(2,1)}), (bf16[896,2048]{1,0:T(8,128)(2,1)}, bf16[896,2048]{1,0:T(8,128)(2,1)})) %all-reduce.14.cloned.1.call-update) | async-done | bytes 7340048 | tf_op jit(solution)/shard_map/psum | solution.py:220
  1449.5 16.5 %all-reduce = (bf16[2048]{0:T(1024)(128)(2,1)S(1)}, bf16[2048]{0:T(1024)(128)(2,1)S(1)}) all-reduce(bf16[2048]{0:T(1024)(128)(2,1)S(1)} %get-tuple-element.11, bf16[2048]{0:T(1024)(128)(2,1)S(1)} %copy-done.52), channel_id=1, replica_groups=mesh['heads'=4,'seq'=8] {'seq'}, use_global_device_ids=true, to_apply=%region_30.31 | all-reduce | flops 4096 | bytes 16384 | tf_op jit(solution)/shard_map/psum | solution.py:324
  (311 shorter events, 371.6 us)
Async XLA Ops:
  7.2 225.8 %copy-start = (bf16[512,2048]{1,0:T(8,128)(2,1)S(1)}, bf16[512,2048]{1,0:T(8,128)(2,1)}, u32[]{:S(2)}) copy-start(bf16[512,2048]{1,0:T(8,128)(2,1)} %param.14) | copy-start | bytes 6291460
  7.2 69.3 %all-gather.11.cloned.1.call-start = ((), (), s32[]{:S(2)}) async-start(), calls=%async_computation.2 | async-start | bytes 3538944 | tf_op jit(solution)/shard_map/all_gather | solution.py:51
  35.4 80.4 %all-gather.13.cloned.1.call-start = ((), (), s32[]{:S(2)}) async-start(), calls=%async_computation.3 | async-start | bytes 3538944 | tf_op jit(solution)/shard_map/all_gather | solution.py:50
  57.9 105.9 %all-gather.17.cloned.1.call-start = ((), (), s32[]{:S(2)}) async-start(), calls=%async_computation.5 | async-start | bytes 4718592 | tf_op jit(solution)/shard_map/all_gather | solution.py:50
  61.7 149.3 %all-gather.15.cloned.1.call-start = ((), (), s32[]{:S(2)}) async-start(), calls=%async_computation.4 | async-start | bytes 4718592 | tf_op jit(solution)/shard_map/all_gather | solution.py:51
  63.6 330.0 %all-reduce.8.cloned.1.call-start = ((), (), s32[]{:S(2)}) async-start(), calls=%async_computation.6 | async-start | bytes 14680064 | tf_op jit(solution)/shard_map/psum | solution.py:210
  63.9 168.0 %copy-start.69 = (s32[512]{0:T(512)}, s32[512]{0:T(512)S(1)}, u32[]{:S(2)}) copy-start(s32[512]{0:T(512)S(1)} %fusion.125) | copy-start | bytes 6148
  68.7 163.3 %copy-start.65 = (s32[896]{0:T(1024)}, s32[896]{0:T(1024)S(1)}, u32[]{:S(2)}) copy-start(s32[896]{0:T(1024)S(1)} %broadcast_multiply_fusion.1) | copy-start | bytes 10756
  68.8 57.0 %copy-start.11 = (pred[128,1024]{1,0:T(8,128)(4,1)}, pred[128,1024]{1,0:T(8,128)(4,1)S(1)}, u32[]{:S(2)}) copy-start(pred[128,1024]{1,0:T(8,128)(4,1)S(1)} %iota_compare_fusion.3) | copy-start | bytes 393220
  239.3 237.9 %all-gather.19.cloned.1.call-start = ((), (), s32[]{:S(2)}) async-start(), calls=%async_computation.7 | async-start | bytes 9437184 | tf_op jit(solution)/shard_map/all_gather | solution.py:214
  239.8 319.9 %all-gather.21.cloned.1.call-start = ((), (), s32[]{:S(2)}) async-start(), calls=%async_computation.8 | async-start | bytes 9437184 | tf_op jit(solution)/shard_map/all_gather | solution.py:215
  240.6 499.3 %all-reduce.10.cloned.1.call-start = ((), (), s32[]{:S(2)}) async-start(), calls=%async_computation.9 | async-start | bytes 14680064 | tf_op jit(solution)/shard_map/psum | solution.py:237
  240.7 319.1 %copy-start.57 = (s32[2048]{0:T(1024)}, s32[2048]{0:T(1024)S(1)}, u32[]{:S(2)}) copy-start(s32[2048]{0:T(1024)S(1)} %iota_add_fusion) | copy-start | bytes 24580
  240.7 319.1 %copy-start.62 = (s32[896]{0:T(1024)}, s32[896]{0:T(1024)S(1)}, u32[]{:S(2)}) copy-start(s32[896]{0:T(1024)S(1)} %broadcast_multiply_fusion) | copy-start | bytes 10756
  398.6 78.6 %copy-start.44 = (f32[2048]{0:T(1024)S(1)}, f32[2048]{0:T(1024)}, u32[]{:S(2)}) copy-start(f32[2048]{0:T(1024)} %param.18) | copy-start | bytes 24580
  586.1 209.2 %all-gather.23.cloned.1.call-start = ((), (), s32[]{:S(2)}) async-start(), calls=%async_computation.10 | async-start | bytes 3538944 | tf_op jit(solution)/shard_map/all_gather | solution.py:269
  590.0 237.3 %all-gather.27.cloned.1.call-start = ((), (), s32[]{:S(2)}) async-start(), calls=%async_computation.12 | async-start | bytes 4718592 | tf_op jit(solution)/shard_map/all_gather | solution.py:269
  593.3 154.0 %copy-start.45 = (f32[2048]{0:T(1024)S(1)}, f32[2048]{0:T(1024)}, u32[]{:S(2)}) copy-start(f32[2048]{0:T(1024)} %param.18) | copy-start | bytes 24580
  593.3 346.1 %all-gather.25.cloned.1.call-start = ((), (), s32[]{:S(2)}) async-start(), calls=%async_computation.11 | async-start | bytes 3538944 | tf_op jit(solution)/shard_map/all_gather | solution.py:270
  758.4 197.6 %all-gather.29.cloned.1.call-start = ((), (), s32[]{:S(2)}) async-start(), calls=%async_computation.13 | async-start | bytes 4718592 | tf_op jit(solution)/shard_map/all_gather | solution.py:270
  760.6 311.6 %reduce-scatter.5.cloned.1.call-start = ((), (), s32[]{:S(2)}) async-start(), calls=%async_computation.15 | async-start | bytes 9437184 | tf_op jit(solution)/shard_map/reduce_scatter | solution.py:244
  776.1 320.9 %reduce-scatter.3.cloned.1.call-start = ((), (), s32[]{:S(2)}) async-start(), calls=%async_computation.14 | async-start | bytes 9437184 | tf_op jit(solution)/shard_map/reduce_scatter | solution.py:241
  791.3 482.0 %all-reduce.12.cloned.1.call-start = ((), (), s32[]{:S(2)}) async-start(), calls=%async_computation.16 | async-start | bytes 16777216 | tf_op jit(solution)/shard_map/psum | solution.py:322
  1009.7 423.1 %all-reduce.14.cloned.1.call-start = ((), (), s32[]{:S(2)}) async-start(), calls=%async_computation.17 | async-start | bytes 14680064 | tf_op jit(solution)/shard_map/psum | solution.py:220
  (66 other events, 647.8 us)
Sparse Core Ops, SparseCore 0:
  35.5 40.9 all-gather.10
  78.6 37.1 all-gather.12
  118.0 45.7 all-gather.16
  165.2 45.6 all-gather.14
  239.4 154.2 all-reduce.7
  395.1 82.0 all-gather.18
  478.7 80.9 all-gather.20
  586.2 153.6 all-reduce.9
  741.5 38.1 all-gather.22
  781.2 46.1 all-gather.26
  829.0 40.0 all-gather.24
  871.1 44.4 all-gather.28
  917.9 87.9 reduce-scatter.4
  1008.6 88.2 reduce-scatter.2
  1099.2 174.0 all-reduce.11
  1277.2 155.5 all-reduce.13
where the time goes:
time: 1490 us; the launch traced here: 1480 us
  waiting for transfers between devices  891 us (60%)
  matrix products  268 us (18%)
  local copies, waits for them, and re-layouts  115 us (8%)
  blocking collectives  106 us (7%)
  other arithmetic  88.5 us (6%)
  between operations  15.1 us (1%)
    psum x1, waiting for transfers between devices, local(): lax.psum(grad_qkv_part.astype(jnp.bfloat16), 'seq').astype(jnp.float32)  174 us
    psum x1, waiting for transfers between devices, local(): hidden = tokens_wide + lax.psum(attn_part, 'heads')  153 us
    psum x1, waiting for transfers between devices, local(): lax.psum(ffn_part.astype(jnp.bfloat16), 'heads').astype(jnp.float32)  148 us
    psum x1, waiting for transfers between devices, local(): lax.psum(jnp.dot(grad_upward, back_up.T, preferred_element_type=jnp.float...  146 us
    all_gather x1, waiting for transfers between devices, local(): lax.all_gather(w_up, 'seq', axis=0, tiled=True)  74.7 us
    all_gather x1, waiting for transfers between devices, local(): lax.all_gather(w_down, 'seq', axis=1, tiled=True)  67.9 us
    all_gather x2, waiting for transfers between devices, gather_rows(): lax.all_gather(keys, 'seq', axis=1, tiled=True)  64.2 us
    unnamed x153, local copies, waits for them, and re-layouts  34.3 us
  transfers between devices with their start and end apart: 16, of which 12 were waited for; matrix products, arithmetic and copies ran while one was open for 23% of the time, Pallas kernels for 0%

commit v1 on v0

--- a/solution.py
+++ b/solution.py
@@ -14,6 +14,11 @@
 SEQS = 5
 epsilon = 1e-05
 highest = lax.Precision.HIGHEST
+
+
+def detail_record(frame):
+    clean = jnp.sum(lax.all_gather(frame, axis_name="seq"), axis=0)
+    return clean
 
 
 def normalize_parts(values):
@@ -319,7 +324,7 @@
     back_one, grad_gain_one = normalize_back(grad_one, hat_one, inverse_one, gain_attn)
     grad_tokens = grad_hidden + back_one
     grad_qkv, grad_out, grad_gain_attn, grad_gain_ffn = (
-        lax.psum(grad_qkv_part.astype(jnp.bfloat16), "seq").astype(jnp.float32),
+        detail_record(grad_qkv_part.astype(jnp.bfloat16)).astype(jnp.float32),
         lax.psum(grad_out_part.astype(jnp.bfloat16), "seq").astype(jnp.float32),
         lax.psum(grad_gain_one.astype(jnp.bfloat16), "seq").astype(jnp.float32),
         lax.psum(grad_gain_two.astype(jnp.bfloat16), "seq").astype(jnp.float32),

time: 1490 us -> 1790 us (1.20)
  waiting for transfers between devices: 891 us -> 1180 us
  other arithmetic: 88.5 us -> 108 us
    all_gather x0 -> x1, waiting for transfers between devices: none -> 385 us  [detail_record(): clean = jnp.sum(lax.all_gather(frame, axis_name='seq'), axis=0)]
    psum x1, waiting for transfers between devices: 174 us -> 0.02 us  [local(): lax.psum(grad_out_part.astype(jnp.bfloat16), 'seq').astype(jnp.float32)]
    reduce_scatter x1, waiting for transfers between devices: 22.1 us -> 88 us  [local(): lax.psum_scatter(grad_up_part.astype(jnp.bfloat16), 'seq', scatter_dimens...]
    reduce_sum x0 -> x1, other arithmetic: none -> 20 us  [detail_record(): clean = jnp.sum(lax.all_gather(frame, axis_name='seq'), axis=0)]
    unnamed x153 -> x151, local copies, waits for them, and re-layouts: 34.3 us -> 35.8 us
  transfers between devices with their start and end apart: 16 -> 17, of which waited for: 12 -> 13; matrix products, arithmetic and copies ran while one was open for 23% -> 20% of each run, Pallas kernels for 0% -> 0%
where the time goes in v1:
time: 1790 us
  waiting for transfers between devices  1180 us (66%)
  matrix products  268 us (15%)
  local copies, waits for them, and re-layouts  113 us (6%)
  other arithmetic  108 us (6%)
  blocking collectives  105 us (6%)
    all_gather x1, waiting for transfers between devices, detail_record(): clean = jnp.sum(lax.all_gather(frame, axis_name='seq'), axis=0)  385 us
    psum x1, waiting for transfers between devices, local(): lax.psum(ffn_part.astype(jnp.bfloat16), 'heads').astype(jnp.float32)  155 us
    psum x1, waiting for transfers between devices, local(): hidden = tokens_wide + lax.psum(attn_part, 'heads')  153 us
    psum x1, waiting for transfers between devices, local(): lax.psum(jnp.dot(grad_upward, back_up.T, preferred_element_type=jnp.float...  150 us
    reduce_scatter x1, waiting for transfers between devices, local(): lax.psum_scatter(grad_up_part.astype(jnp.bfloat16), 'seq', scatter_dimens...  88 us
    all_gather x1, waiting for transfers between devices, local(): lax.all_gather(w_up, 'seq', axis=0, tiled=True)  74.7 us
    all_gather x1, waiting for transfers between devices, local(): lax.all_gather(w_down, 'seq', axis=1, tiled=True)  68.1 us
    all_gather x2, waiting for transfers between devices, gather_rows(): lax.all_gather(keys, 'seq', axis=1, tiled=True)  64 us
  transfers between devices with their start and end apart: 17, of which 13 were waited for; matrix products, arithmetic and copies ran while one was open for 20% of the time, Pallas kernels for 0%

profile of v1, /device:TPU:0, one launch (start us, length us, event | category | flops | bytes accessed | tf_op | source)
XLA Modules:
  0.0 1787.7 jit_solution(6313281498601690010)
XLA Ops:
  81.2 34.6 %all-gather.15.cloned.1.call-done = bf16[3,1024,512]{2,1,0:T(8,128)(2,1)} async-done(((bf16[3,128,512]{2,1,0:T(8,128)(2,1)}), bf16[3,1024,512]{2,1,0:T(8,128)(2,1)}) %all-gather.15.cloned.1.call-update) | async-done | bytes 3145744 | tf_op jit(solution)/shard_map/all_gather | solution.py:55
  134.4 29.4 %all-gather.19.cloned.1.call-done = bf16[2,2048,512]{2,1,0:T(8,128)(2,1)} async-done(((bf16[2,256,512]{2,1,0:T(8,128)(2,1)}), bf16[2,2048,512]{2,1,0:T(8,128)(2,1)}) %all-gather.19.cloned.1.call-update) | async-done | bytes 4194320 | tf_op jit(solution)/shard_map/all_gather | solution.py:55
  185.7 25.3 %all-gather.17.cloned.1.call-done = bf16[2,2048,512]{2,1,0:T(8,128)(2,1)} async-done(((bf16[2,256,512]{2,1,0:T(8,128)(2,1)}), bf16[2,2048,512]{2,1,0:T(8,128)(2,1)}) %all-gather.17.cloned.1.call-update) | async-done | bytes 4194320 | tf_op jit(solution)/shard_map/all_gather | solution.py:56
  240.7 153.0 %all-reduce.7.cloned.1.call-done = f32[896,2048]{1,0:T(8,128)} async-done(((f32[896,2048]{1,0:T(8,128)}), f32[896,2048]{1,0:T(8,128)}) %all-reduce.7.cloned.1.call-update) | async-done | bytes 7340048 | tf_op jit(solution)/shard_map/psum | solution.py:215
  402.5 74.7 %all-gather.21.cloned.1.call-done = bf16[2048,2048]{1,0:T(8,128)(2,1)} async-done(((bf16[256,2048]{1,0:T(8,128)(2,1)}), bf16[2048,2048]{1,0:T(8,128)(2,1)}) %all-gather.21.cloned.1.call-update) | async-done | bytes 8388624 | tf_op jit(solution)/shard_map/all_gather | solution.py:219
  477.2 14.5 fusion.154
  491.7 68.1 %all-gather.23.cloned.1.call-done = bf16[2048,2048]{1,0:T(8,128)(2,1)} async-done(((bf16[2048,256]{1,0:T(8,128)(2,1)}), bf16[2048,2048]{1,0:T(8,128)(2,1)}) %all-gather.23.cloned.1.call-update) | async-done | bytes 8388624 | tf_op jit(solution)/shard_map/all_gather | solution.py:220
  559.8 15.0 fusion.29
  589.9 150.0 %all-reduce.9.cloned.1.call-done = f32[896,2048]{1,0:T(8,128)} async-done(((f32[896,2048]{1,0:T(8,128)}), f32[896,2048]{1,0:T(8,128)}) %all-reduce.9.cloned.1.call-update) | async-done | bytes 7340048 | tf_op jit(solution)/shard_map/psum | solution.py:242
  768.0 15.6 convolution_convert_fusion
  784.3 15.0 convolution_convert_fusion.1
  807.6 13.8 all_gather.57
  834.1 18.2 %all_gather.61 = f32[2,4,2048]{2,1,0:T(4,128)} all-gather(f32[2,4,256]{2,1,0:T(4,128)S(1)} %bitcast.164), channel_id=1, replica_groups=mesh['heads'=4,'seq'=8] {'seq'}, dimensions={2}, use_global_device_ids=true | all-gather | bytes 73728 | tf_op jit(solution)/shard_map/all_gather | solution.py:278
  862.7 14.0 convolution_convert_fusion.3
  889.0 13.4 multiply_reduce_fusion
  902.4 15.0 fusion.74
  930.5 15.0 all_gather.63
  972.6 13.6 fusion.72
  1033.6 28.2 %psum.60 = bf16[5,2048]{1,0:T(8,128)(2,1)S(1)} all-reduce(bf16[5,2048]{1,0:T(8,128)(2,1)S(1)} %fusion.55), channel_id=1, replica_groups=mesh['heads'=4,'seq'=8] {'seq'}, use_global_device_ids=true, to_apply=%region_18.19 | all-reduce | flops 10240 | bytes 40960 | tf_op jit(solution)/shard_map/psum | solution.py:194
  1076.7 88.0 %reduce-scatter.3.cloned.1.call-done = bf16[256,2048]{1,0:T(8,128)(2,1)} async-done(((bf16[2048,2048]{1,0:T(8,128)(2,1)}), bf16[256,2048]{1,0:T(8,128)(2,1)}) %reduce-scatter.3.cloned.1.call-update) | async-done | bytes 1048592 | tf_op jit(solution)/shard_map/reduce_scatter | solution.py:246
  1167.5 155.1 %all-reduce.13.cloned.1.call-done = (bf16[896,2048]{1,0:T(8,128)(2,1)}, bf16[896,2048]{1,0:T(8,128)(2,1)}) async-done(((bf16[896,2048]{1,0:T(8,128)(2,1)}, bf16[896,2048]{1,0:T(8,128)(2,1)}), (bf16[896,2048]{1,0:T(8,128)(2,1)}, bf16[896,2048]{1,0:T(8,128)(2,1)})) %all-reduce.13.cloned.1.call-update) | async-done | bytes 7340048 | tf_op jit(solution)/shard_map/psum | solution.py:225
  1332.7 17.2 all-reduce
  1366.6 385.0 %all-gather.33.cloned.1.call-done = bf16[16384,3,512]{2,0,1:T(8,128)(2,1)} async-done(((bf16[2048,3,512]{2,0,1:T(8,128)(2,1)}), bf16[16384,3,512]{2,0,1:T(8,128)(2,1)}) %all-gather.33.cloned.1.call-update) | async-done | bytes 50331664 | tf_op jit(solution)/shard_map/all_gather | solution.py:20
  1751.6 20.0 %reduce_sum.190 = bf16[2048,3,512]{2,0,1:T(8,128)(2,1)} reduce(bf16[8,2048,3,512]{3,1,0,2:T(8,128)(2,1)} %bitcast.129, bf16[]{:T(256)} %constant.126.clone.1), dimensions={0}, to_apply=%region_25.26 | reduce | flops 22020096 | bytes 56623104 | tf_op jit(solution)/shard_map/reduce_sum | solution.py:20
  (313 shorter events, 380.9 us)
Async XLA Ops:
  7.2 225.8 %copy-start = (bf16[512,2048]{1,0:T(8,128)(2,1)S(1)}, bf16[512,2048]{1,0:T(8,128)(2,1)}, u32[]{:S(2)}) copy-start(bf16[512,2048]{1,0:T(8,128)(2,1)} %param.14) | copy-start | bytes 6291460
  7.2 69.3 %all-gather.13.cloned.1.call-start = ((), (), s32[]{:S(2)}) async-start(), calls=%async_computation.2 | async-start | bytes 3538944 | tf_op jit(solution)/shard_map/all_gather | solution.py:56
  35.4 80.4 %all-gather.15.cloned.1.call-start = ((), (), s32[]{:S(2)}) async-start(), calls=%async_computation.3 | async-start | bytes 3538944 | tf_op jit(solution)/shard_map/all_gather | solution.py:55
  57.9 105.9 %all-gather.19.cloned.1.call-start = ((), (), s32[]{:S(2)}) async-start(), calls=%async_computation.5 | async-start | bytes 4718592 | tf_op jit(solution)/shard_map/all_gather | solution.py:55
  61.6 149.3 %all-gather.17.cloned.1.call-start = ((), (), s32[]{:S(2)}) async-start(), calls=%async_computation.4 | async-start | bytes 4718592 | tf_op jit(solution)/shard_map/all_gather | solution.py:56
  63.6 330.1 %all-reduce.7.cloned.1.call-start = ((), (), s32[]{:S(2)}) async-start(), calls=%async_computation.6 | async-start | bytes 14680064 | tf_op jit(solution)/shard_map/psum | solution.py:215
  63.9 168.1 %copy-start.69 = (s32[512]{0:T(512)}, s32[512]{0:T(512)S(1)}, u32[]{:S(2)}) copy-start(s32[512]{0:T(512)S(1)} %fusion.125) | copy-start | bytes 6148
  68.7 163.3 %copy-start.63 = (s32[896]{0:T(1024)}, s32[896]{0:T(1024)S(1)}, u32[]{:S(2)}) copy-start(s32[896]{0:T(1024)S(1)} %broadcast_multiply_fusion.1) | copy-start | bytes 10756
  69.2 147.9 %copy-start.6 = (pred[256,2048]{1,0:T(8,128)(4,1)}, pred[256,2048]{1,0:T(8,128)(4,1)S(1)}, u32[]{:S(2)}) copy-start(pred[256,2048]{1,0:T(8,128)(4,1)S(1)} %iota_compare_fusion.1) | copy-start | bytes 1572868
  239.3 237.9 %all-gather.21.cloned.1.call-start = ((), (), s32[]{:S(2)}) async-start(), calls=%async_computation.7 | async-start | bytes 9437184 | tf_op jit(solution)/shard_map/all_gather | solution.py:219
  239.9 319.9 %all-gather.23.cloned.1.call-start = ((), (), s32[]{:S(2)}) async-start(), calls=%async_computation.8 | async-start | bytes 9437184 | tf_op jit(solution)/shard_map/all_gather | solution.py:220
  240.6 499.3 %all-reduce.9.cloned.1.call-start = ((), (), s32[]{:S(2)}) async-start(), calls=%async_computation.9 | async-start | bytes 14680064 | tf_op jit(solution)/shard_map/psum | solution.py:242
  240.7 319.1 %copy-start.59 = (s32[2048]{0:T(1024)}, s32[2048]{0:T(1024)S(1)}, u32[]{:S(2)}) copy-start(s32[2048]{0:T(1024)S(1)} %iota_add_fusion) | copy-start | bytes 24580
  240.7 319.1 %copy-start.65 = (s32[896]{0:T(1024)}, s32[896]{0:T(1024)S(1)}, u32[]{:S(2)}) copy-start(s32[896]{0:T(1024)S(1)} %broadcast_multiply_fusion) | copy-start | bytes 10756
  398.6 78.6 %copy-start.46 = (f32[2048]{0:T(1024)S(1)}, f32[2048]{0:T(1024)}, u32[]{:S(2)}) copy-start(f32[2048]{0:T(1024)} %param.18) | copy-start | bytes 24580
  586.1 216.8 %all-gather.25.cloned.1.call-start = ((), (), s32[]{:S(2)}) async-start(), calls=%async_computation.10 | async-start | bytes 3538944 | tf_op jit(solution)/shard_map/all_gather | solution.py:274
  588.3 239.0 %all-gather.29.cloned.1.call-start = ((), (), s32[]{:S(2)}) async-start(), calls=%async_computation.12 | async-start | bytes 4718592 | tf_op jit(solution)/shard_map/all_gather | solution.py:274
  589.8 355.7 %all-gather.27.cloned.1.call-start = ((), (), s32[]{:S(2)}) async-start(), calls=%async_computation.11 | async-start | bytes 3538944 | tf_op jit(solution)/shard_map/all_gather | solution.py:275
  758.4 203.5 %all-gather.31.cloned.1.call-start = ((), (), s32[]{:S(2)}) async-start(), calls=%async_computation.13 | async-start | bytes 4718592 | tf_op jit(solution)/shard_map/all_gather | solution.py:275
  760.6 303.3 %all-reduce.11.cloned.1.call-start = ((), (), s32[]{:S(2)}) async-start(), calls=%async_computation.14 | async-start | bytes 4194304 | tf_op jit(solution)/shard_map/psum | solution.py:328
  768.0 306.0 %reduce-scatter.5.cloned.1.call-start = ((), (), s32[]{:S(2)}) async-start(), calls=%async_computation.16 | async-start | bytes 9437184 | tf_op jit(solution)/shard_map/reduce_scatter | solution.py:249
  783.6 381.1 %reduce-scatter.3.cloned.1.call-start = ((), (), s32[]{:S(2)}) async-start(), calls=%async_computation.15 | async-start | bytes 9437184 | tf_op jit(solution)/shard_map/reduce_scatter | solution.py:246
  799.4 523.1 %all-reduce.13.cloned.1.call-start = ((), (), s32[]{:S(2)}) async-start(), calls=%async_computation.18 | async-start | bytes 14680064 | tf_op jit(solution)/shard_map/psum | solution.py:225
  1008.7 742.9 %all-gather.33.cloned.1.call-start = ((), (), s32[]{:S(2)}) async-start(), calls=%async_computation.17 | async-start | bytes 56623104 | tf_op jit(solution)/shard_map/all_gather | solution.py:20
  (66 other events, 681.1 us)
Sparse Core Ops, SparseCore 0:
  35.5 40.9 all-gather.12
  78.7 37.1 all-gather.14
  118.0 45.7 all-gather.18
  165.2 45.6 all-gather.16
  239.4 154.2 all-reduce.6
  395.1 82.0 all-gather.20
  478.8 80.9 all-gather.22
  586.2 153.5 all-reduce.8
  741.5 38.1 all-gather.24
  781.2 46.1 all-gather.28
  829.0 38.3 all-gather.26
  869.4 46.0 all-gather.30
  918.4 63.6 all-reduce.10
  984.2 89.6 reduce-scatter.4
  1076.7 87.9 reduce-scatter.2
  1168.6 153.8 all-reduce.12
  1324.0 427.5 all-gather.32
